TPU v7x, 512 devices: a whole 4x4x16 slice. The times are simulated.
512 devices in a mesh: feat: 8 (over z_lo), lat: 64 (over y, z_hi, x, core).
Axes of the slice: x: 4, y: 4, z: 16 (z_hi: 2, z_lo: 8; z = z_hi * 8 + z_lo), core: 2. Of those that a mesh axis runs over, the one named last changes fastest.
Arguments:
- acts: bfloat16 [2, 512, 4096], P(None, 'lat', 'feat'), may hold values from -6 to 6
- weight: bfloat16 [2, 4096, 65536], P(None, 'feat', 'lat'), may hold values from -0.0625 to 0.0625
- enc_bias: float32 [65536], P('lat'), may hold values from -1 to 0.5
- dec_bias: float32 [2, 4096], P(None, 'feat'), may hold values from -1 to 1
Outputs:
- grad_weight: bfloat16 [2, 4096, 65536], P(None, 'feat', 'lat')
- grad_enc_bias: float32 [65536], P('lat')
- grad_dec_bias: float32 [2, 4096], P(None, 'feat')
All inputs are finite; a program needn't handle non-finite values.
Results may differ from a plain program's by a relative error of at most 0.0085.
Values may be sent and summed in bfloat16 or wider, within the bound.
A program may use at most 64 MiB of HBM per device.

v0:
```python
import math
import jax
import jax.numpy as jnp
from jax import lax
from jax.sharding import Mesh
from jax.sharding import PartitionSpec as P

LAT = ("lat_0", "lat_1", "lat_2", "lat_3")


def in_blocks(shard, dim, count):
    dims = shard.shape
    blocks = shard.reshape(*dims[:dim], count, dims[dim] // count, *dims[dim + 1 :])
    return jnp.moveaxis(blocks, dim, 0)


def summed_on_arrival(shard, axis, dim):
    blocks = in_blocks(shard, dim, lax.axis_size(axis))
    arrived = lax.all_to_all(blocks, axis, split_axis=0, concat_axis=0, tiled=True)
    return arrived.astype(jnp.float32).sum(axis=0)


def in_order(blocks, dim):
    dims = list(blocks.shape[1:])
    dims[dim] *= blocks.shape[0]
    return jnp.moveaxis(blocks, 0, dim).reshape(dims)


def from_everyone(shard, axis):
    copies = jnp.broadcast_to(shard, (lax.axis_size(axis), *shard.shape))
    return lax.all_to_all(copies, axis, split_axis=0, concat_axis=0, tiled=True)


def gathered_copies(shard, axis, dim):
    return in_order(from_everyone(shard, axis), dim)


def sum_at_owner(shard, axis, dim):
    count = lax.axis_size(axis)
    blocks = lax.all_to_all(in_blocks(shard, dim, count), axis, 0, 0, tiled=True)
    return jnp.sum(blocks, axis=0)


def sum_by_axis(shard, axes, dim):
    far, near = axes
    blocks = in_blocks(shard, dim, lax.axis_size(far))
    nearer = sum_at_owner(blocks, near, dim + 1)
    arrived = lax.all_to_all(nearer, far, split_axis=0, concat_axis=0, tiled=True)
    return arrived.sum(axis=0)


def filled_up(lines, count):
    spare = -len(lines) % count
    return jnp.pad(lines, [(0, spare)] + [(0, 0)] * (lines.ndim - 1))


def gathered_by_axis(shard, axes, dim):
    far, near = axes
    blocks = from_everyone(from_everyone(shard, far), near)
    return in_order(blocks.swapaxes(0, 1).reshape(-1, *shard.shape), dim)


def nested_sum(shard, axes):
    lines = shard.reshape(-1, shard.shape[-1])
    own = sum_by_axis(filled_up(lines, lax.axis_size(axes[0]) * lax.axis_size(axes[1])), axes, 0)
    whole = gathered_by_axis(own, axes, 0)
    return whole[: len(lines)].reshape(shard.shape)


def taken_together(shard, axis):
    everything = from_everyone(shard, axis)
    return jnp.sum(everything, axis=0)


def channel_terms(left, right):
    first = jnp.dot(left[0], right[0], preferred_element_type=jnp.float32)
    return first + jnp.dot(left[1], right[1], preferred_element_type=jnp.float32)


def on_device(acts, weight, enc_bias, dec_bias):
    width = weight.shape[1] * lax.axis_size("feat")
    lats = weight.shape[2] * lax.axis_size(LAT)
    scale = math.sqrt(2.0 * width / lats)
    whole_rows = lax.all_gather(acts, LAT, axis=1, tiled=True)
    partial_value = channel_terms(whole_rows, weight)
    pre_share = summed_on_arrival(partial_value.astype(jnp.bfloat16), "feat", 0) + enc_bias
    act_share = jax.nn.softplus(pre_share).astype(jnp.bfloat16)
    latents = gathered_copies(act_share, "feat", 0)
    recon_terms = jnp.einsum("rl,mdl->mrd", latents, weight, preferred_element_type=jnp.float32)
    summed = nested_sum(recon_terms, (("lat_0", "lat_1", "lat_2"), "lat_3"))
    resid = scale * summed + dec_bias[:, None, :] - whole_rows.astype(jnp.float32)
    grad_dec_bias = jnp.sum(resid, axis=1)
    resid_rows = resid.astype(jnp.bfloat16)
    backed = channel_terms(resid_rows, weight)
    back_part = summed_on_arrival(backed.astype(jnp.bfloat16), "feat", 0)
    grad_share = scale * back_part * jax.nn.sigmoid(pre_share)
    grad_enc_bias = taken_together(jnp.sum(grad_share, axis=0), "feat")
    grad_pre_b = gathered_copies(grad_share.astype(jnp.bfloat16), "feat", 0)
    enc_term = jnp.einsum("mrd,rl->mdl", whole_rows, grad_pre_b, preferred_element_type=jnp.float32)
    dec_term = jnp.einsum("mrd,rl->mdl", resid_rows, latents, preferred_element_type=jnp.float32)
    grad_weight = (enc_term + scale * dec_term).astype(jnp.bfloat16)
    return (grad_weight, grad_enc_bias, grad_dec_bias)


def solution(mesh):
    torus = Mesh(
        mesh.devices.reshape(mesh.shape["feat"], 4, 2, 4, 2),
        ("feat", "lat_0", "lat_1", "lat_2", "lat_3"),
    )
    in_specs = (P(None, LAT, "feat"), P(None, "feat", LAT), P(LAT), P(None, "feat"))
    out_specs = (P(None, "feat", LAT), P(LAT), P(None, "feat"))
    return jax.shard_map(
        on_device, mesh=torus, in_specs=in_specs, out_specs=out_specs, check_vma=False
    )
```

profile of v0, /device:TPU:2, one launch (start us, length us, event | category | flops | bytes accessed | tf_op | source)
XLA Modules:
  0.0 509.9 jit_solution(4687224585062646519)
XLA Ops:
  7.2 0.7 all-gather.2.cloned.1.call-update
  7.9 110.8 %all-gather.2.cloned.1.call-done = bf16[2,512,512]{2,1,0:T(8,128)(2,1)} async-done(((bf16[2,8,512]{2,1,0:T(8,128)(2,1)}), bf16[2,512,512]{2,1,0:T(8,128)(2,1)}) %all-gather.2.cloned.1.call-update) | async-done | bytes 1048592 | tf_op jit(solution)/shard_map/all_gather | solution.py:84
  118.8 2.2 fusion.7
  121.0 0.7 add_convert_fusion.1
  121.7 54.3 %all_to_all.46 = bf16[8,64,1024]{2,1,0:T(8,128)(2,1)S(1)} all-to-all(bf16[8,64,1024]{2,1,0:T(8,128)(2,1)S(1)} %bitcast.52), channel_id=1, replica_groups=mesh['feat'=8,'lat_0'=4,'lat_1'=2,'lat_2'=4,'lat_3'=2] {'feat'}, dimensions={0} | all-to-all | bytes 2097152 | tf_op jit(solution)/shard_map/all_to_all | solution.py:19
  176.5 55.2 %all_to_all.47 = bf16[8,64,1024]{2,1,0:T(8,128)(2,1)S(1)} all-to-all(bf16[8,64,1024]{2,1,0:T(8,128)(2,1)S(1)} %broadcast_in_dim.17), channel_id=1, replica_groups=mesh['feat'=8,'lat_0'=4,'lat_1'=2,'lat_2'=4,'lat_3'=2] {'feat'}, dimensions={0} | all-to-all | bytes 2097152 | tf_op jit(solution)/shard_map/all_to_all | solution.py:31
  231.7 1.3 fusion.15
  233.3 5.4 %all_to_all.48 = f32[2,32,16,512]{3,2,1,0:T(8,128)S(1)} all-to-all(f32[2,32,16,512]{3,2,1,0:T(8,128)S(1)} %bitcast.50), channel_id=1, replica_groups=mesh['feat'=8,'lat_0'=4,'lat_1'=2,'lat_2'=4,'lat_3'=2] {'lat_3'}, dimensions={0} | all-to-all | bytes 4194304 | tf_op jit(solution)/shard_map/all_to_all | solution.py:40
  238.7 1.3 reduce_sum.64
  239.9 60.7 %all_to_all.49 = f32[32,16,512]{2,1,0:T(8,128)S(1)} all-to-all(f32[32,16,512]{2,1,0:T(8,128)} %reduce_sum.64), channel_id=1, replica_groups=mesh['feat'=8,'lat_0'=4,'lat_1'=2,'lat_2'=4,'lat_3'=2] {'lat_0','lat_1',..., dimensions={0} | all-to-all | bytes 2097152 | tf_op jit(solution)/shard_map/all_to_all | solution.py:48
  300.8 50.3 %all_to_all.50 = f32[32,16,512]{2,1,0:T(8,128)S(1)} all-to-all(f32[32,16,512]{2,1,0:T(8,128)S(1)} %broadcast_in_dim.18), channel_id=1, replica_groups=mesh['feat'=8,'lat_0'=4,'lat_1'=2,'lat_2'=4,'lat_3'=2] {'lat_0','lat_1',..., dimensions={0} | all-to-all | bytes 2097152 | tf_op jit(solution)/shard_map/all_to_all | solution.py:31
  351.3 5.4 %all_to_all.51 = f32[2,32,16,512]{3,2,1,0:T(8,128)S(1)} all-to-all(f32[2,32,16,512]{3,2,1,0:T(8,128)S(1)} %broadcast_in_dim.19), channel_id=1, replica_groups=mesh['feat'=8,'lat_0'=4,'lat_1'=2,'lat_2'=4,'lat_3'=2] {'lat_3'}, dimensions={0} | all-to-all | bytes 4194304 | tf_op jit(solution)/shard_map/all_to_all | solution.py:31
  357.7 1.0 fusion.1
  359.3 0.7 fusion.5
  360.0 0.7 add_convert_fusion
  360.7 65.0 %all_to_all.52 = bf16[8,64,1024]{2,1,0:T(8,128)(2,1)S(1)} all-to-all(bf16[8,64,1024]{2,1,0:T(8,128)(2,1)S(1)} %bitcast.53), channel_id=1, replica_groups=mesh['feat'=8,'lat_0'=4,'lat_1'=2,'lat_2'=4,'lat_3'=2] {'feat'}, dimensions={0} | all-to-all | bytes 2097152 | tf_op jit(solution)/shard_map/all_to_all | solution.py:19
  426.0 14.7 %all_to_all.53 = f32[8,1,1024]{2,1,0:T(1,128)S(1)} all-to-all(f32[8,1,1024]{2,1,0:T(1,128)S(1)} %broadcast_in_dim.21), channel_id=1, replica_groups=mesh['feat'=8,'lat_0'=4,'lat_1'=2,'lat_2'=4,'lat_3'=2] {'feat'}, dimensions={0} | all-to-all | bytes 65536 | tf_op jit(solution)/shard_map/all_to_all | solution.py:31
  440.7 1.1 broadcast_in_dim.20
  441.8 3.6 all-to-all-start.7
  445.4 0.6 reduce_sum.68
  446.0 49.1 %all-to-all-done.7 = bf16[8,64,1024]{2,1,0:T(8,128)(2,1)S(1)} async-done(((bf16[8,64,1024]{2,1,0:T(8,128)(2,1)}), bf16[8,64,1024]{2,1,0:T(8,128)(2,1)S(1)}, u32[]{:S(2)}, u32[]{:S(2)}) %all-to-all-start.7) | async-done | bytes 1048608 | tf_op jit(solution)/shard_map/all_to_all | solution.py:31
  495.1 1.3 fusion.16
  496.4 2.8 fusion
  499.1 3.9 copy.33
  (27 shorter events, 3.0 us)
Async XLA Ops:
  7.2 113.8 %copy-start.1 = (bf16[2,512,1024]{2,1,0:T(8,128)(2,1)S(1)}, bf16[2,512,1024]{2,1,0:T(8,128)(2,1)}, u32[]{:S(2)}) copy-start(bf16[2,512,1024]{2,1,0:T(8,128)(2,1)} %param.5) | copy-start | bytes 6291460
  7.2 111.6 %all-gather.2.cloned.1.call-start = ((), (), s32[]{:S(2)}) async-start(), calls=%async_computation.9 | async-start | bytes 1064960 | tf_op jit(solution)/shard_map/all_gather | solution.py:84
  118.8 2.2 copy-start
  121.7 54.5 %copy-start.5 = (f32[1024]{0:T(1024)S(1)}, f32[1024]{0:T(1024)}, u32[]{:S(2)}) copy-start(f32[1024]{0:T(1024)} %param.6) | copy-start | bytes 12292
  231.7 1.3 copy-start.3
  357.0 0.7 copy-start.6
  357.7 1.6 copy-start.2
  441.8 53.3 %all-to-all-start.7 = ((bf16[8,64,1024]{2,1,0:T(8,128)(2,1)}), bf16[8,64,1024]{2,1,0:T(8,128)(2,1)S(1)}, u32[]{:S(2)}, u32[]{:S(2)}) async-start(bf16[8,64,1024]{2,1,0:T(8,128)(2,1)} %broadcast_in_dim.20), calls=%async_computation.7 | async-start | bytes 2097152 | tf_op jit(solution)/shard_map/all_to_all | solution.py:31
  495.1 1.3 copy-start.4
Sparse Core Ops, SparseCore 0:
  12.2 106.4 all-gather.1
where the time goes:
time: 511 us; the launch traced here: 510 us
  blocking collectives  311 us (61%)
  waiting for transfers between devices  161 us (32%)
  between operations  14.2 us (3%)
  matrix products  9.68 us (2%)
  local copies, waits for them, and re-layouts  7.09 us (1%)
    all_to_all x4, blocking collectives, from_everyone(): return lax.all_to_all(copies, axis, split_axis=0, concat_axis=0, tiled=True)  126 us
    all_to_all x2, blocking collectives, summed_on_arrival(): lax.all_to_all(blocks, axis, split_axis=0, concat_axis=0, tiled=True)  119 us
    all_gather x1, waiting for transfers between devices, on_device(): whole_rows = lax.all_gather(acts, LAT, axis=1, tiled=True)  111 us
    all_to_all x1, blocking collectives, sum_by_axis(): lax.all_to_all(nearer, far, split_axis=0, concat_axis=0, tiled=True)  60.7 us
    all_to_all x1, waiting for transfers between devices, from_everyone(): return lax.all_to_all(copies, axis, split_axis=0, concat_axis=0, tiled=True)  49.1 us
  transfers between devices with their start and end apart: 2, of which 2 were waited for; matrix products, arithmetic and copies ran while one was open for 0% of the time, Pallas kernels for 0%

commit v1 on v0

--- a/solution.py
+++ b/solution.py
@@ -81,7 +81,9 @@
     width = weight.shape[1] * lax.axis_size("feat")
     lats = weight.shape[2] * lax.axis_size(LAT)
     scale = math.sqrt(2.0 * width / lats)
-    whole_rows = lax.all_gather(acts, LAT, axis=1, tiled=True)
+    whole_rows = jnp.concatenate(
+        lax.all_to_all(jnp.stack([acts] * lax.axis_size(LAT)), LAT, 0, 0), axis=1
+    )
     partial_value = channel_terms(whole_rows, weight)
     pre_share = summed_on_arrival(partial_value.astype(jnp.bfloat16), "feat", 0) + enc_bias
     act_share = jax.nn.softplus(pre_share).astype(jnp.bfloat16)

time: 511 us -> 461 us (0.902)
  waiting for transfers between devices: 161 us -> 46.2 us
  blocking collectives: 311 us -> 387 us
  between operations: 14.2 us -> 0.83 us
    all_gather x1 -> x0, waiting for transfers between devices: 111 us -> none  [on_device(): whole_rows = lax.all_gather(acts, LAT, axis=1, tiled=True)]
    all_to_all x0 -> x1, blocking collectives: none -> 52.1 us  [on_device(): lax.all_to_all(jnp.stack([acts] * lax.axis_size(LAT)), LAT, 0, 0)]
    all_to_all x2, blocking collectives: 119 us -> 148 us  [summed_on_arrival(): lax.all_to_all(blocks, axis, split_axis=0, concat_axis=0, tiled=True)]
    all_to_all x1, blocking collectives: 60.7 us -> 55.5 us  [sum_by_axis(): lax.all_to_all(nearer, far, split_axis=0, concat_axis=0, tiled=True)]
  transfers between devices with their start and end apart: 2 -> 1, of which waited for: 2 -> 1; matrix products, arithmetic and copies ran while one was open for 0% -> 1% of each run, Pallas kernels for 0% -> 0%
where the time goes in v1:
time: 461 us; the launch traced here: 460 us
  blocking collectives  387 us (84%)
  waiting for transfers between devices  46.2 us (10%)
  matrix products  8.25 us (2%)
  local copies, waits for them, and re-layouts  7.09 us (2%)
  other arithmetic  5.73 us (1%)
    all_to_all x2, blocking collectives, summed_on_arrival(): lax.all_to_all(blocks, axis, split_axis=0, concat_axis=0, tiled=True)  148 us
    all_to_all x4, blocking collectives, from_everyone(): return lax.all_to_all(copies, axis, split_axis=0, concat_axis=0, tiled=True)  126 us
    all_to_all x1, blocking collectives, sum_by_axis(): lax.all_to_all(nearer, far, split_axis=0, concat_axis=0, tiled=True)  55.5 us
    all_to_all x1, blocking collectives, on_device(): lax.all_to_all(jnp.stack([acts] * lax.axis_size(LAT)), LAT, 0, 0)  52.1 us
    all_to_all x1, waiting for transfers between devices, from_everyone(): return lax.all_to_all(copies, axis, split_axis=0, concat_axis=0, tiled=True)  46.2 us
  transfers between devices with their start and end apart: 1, of which 1 were waited for; matrix products, arithmetic and copies ran while one was open for 1% of the time, Pallas kernels for 0%

profile of v1, /device:TPU:2, one launch (start us, length us, event | category | flops | bytes accessed | tf_op | source)
XLA Modules:
  0.0 459.9 jit_solution(1010326856465870960)
XLA Ops:
  0.6 1.0 stack.2
  1.6 52.1 %all_to_all.51 = bf16[64,2,8,512]{3,2,1,0:T(8,128)(2,1)S(1)} all-to-all(bf16[64,2,8,512]{3,2,1,0:T(8,128)(2,1)S(1)} %stack.2), channel_id=1, replica_groups=mesh['feat'=8,'lat_0'=4,'lat_1'=2,'lat_2'=4,'lat_3'=2] {'lat_0','lat_1',..., dimensions={0} | all-to-all | bytes 2097152 | tf_op jit(solution)/shard_map/all_to_all | solution.py:85
  53.8 0.7 fusion.7
  54.5 0.7 add_convert_fusion.1
  55.2 83.2 %all_to_all.52 = bf16[8,64,1024]{2,1,0:T(8,128)(2,1)S(1)} all-to-all(bf16[8,64,1024]{2,1,0:T(8,128)(2,1)S(1)} %bitcast.76), channel_id=1, replica_groups=mesh['feat'=8,'lat_0'=4,'lat_1'=2,'lat_2'=4,'lat_3'=2] {'feat'}, dimensions={0} | all-to-all | bytes 2097152 | tf_op jit(solution)/shard_map/all_to_all | solution.py:19
  138.9 54.9 %all_to_all.53 = bf16[8,64,1024]{2,1,0:T(8,128)(2,1)S(1)} all-to-all(bf16[8,64,1024]{2,1,0:T(8,128)(2,1)S(1)} %broadcast_in_dim.17), channel_id=1, replica_groups=mesh['feat'=8,'lat_0'=4,'lat_1'=2,'lat_2'=4,'lat_3'=2] {'feat'}, dimensions={0} | all-to-all | bytes 2097152 | tf_op jit(solution)/shard_map/all_to_all | solution.py:31
  193.8 1.3 fusion.18
  195.4 5.4 %all_to_all.54 = f32[2,32,16,512]{3,2,1,0:T(8,128)S(1)} all-to-all(f32[2,32,16,512]{3,2,1,0:T(8,128)S(1)} %bitcast.73), channel_id=1, replica_groups=mesh['feat'=8,'lat_0'=4,'lat_1'=2,'lat_2'=4,'lat_3'=2] {'lat_3'}, dimensions={0} | all-to-all | bytes 4194304 | tf_op jit(solution)/shard_map/all_to_all | solution.py:40
  200.8 1.3 reduce_sum.71
  202.1 55.5 %all_to_all.55 = f32[32,16,512]{2,1,0:T(8,128)S(1)} all-to-all(f32[32,16,512]{2,1,0:T(8,128)} %reduce_sum.71), channel_id=1, replica_groups=mesh['feat'=8,'lat_0'=4,'lat_1'=2,'lat_2'=4,'lat_3'=2] {'lat_0','lat_1',..., dimensions={0} | all-to-all | bytes 2097152 | tf_op jit(solution)/shard_map/all_to_all | solution.py:48
  257.8 51.3 %all_to_all.56 = f32[32,16,512]{2,1,0:T(8,128)S(1)} all-to-all(f32[32,16,512]{2,1,0:T(8,128)S(1)} %broadcast_in_dim.18), channel_id=1, replica_groups=mesh['feat'=8,'lat_0'=4,'lat_1'=2,'lat_2'=4,'lat_3'=2] {'lat_0','lat_1',..., dimensions={0} | all-to-all | bytes 2097152 | tf_op jit(solution)/shard_map/all_to_all | solution.py:31
  309.4 5.4 %all_to_all.57 = f32[2,32,16,512]{3,2,1,0:T(8,128)S(1)} all-to-all(f32[2,32,16,512]{3,2,1,0:T(8,128)S(1)} %broadcast_in_dim.19), channel_id=1, replica_groups=mesh['feat'=8,'lat_0'=4,'lat_1'=2,'lat_2'=4,'lat_3'=2] {'lat_3'}, dimensions={0} | all-to-all | bytes 4194304 | tf_op jit(solution)/shard_map/all_to_all | solution.py:31
  315.9 1.2 copy-done.1
  317.1 0.7 fusion.5
  317.8 0.7 add_convert_fusion
  318.5 64.7 %all_to_all.58 = bf16[8,64,1024]{2,1,0:T(8,128)(2,1)S(1)} all-to-all(bf16[8,64,1024]{2,1,0:T(8,128)(2,1)S(1)} %bitcast.75), channel_id=1, replica_groups=mesh['feat'=8,'lat_0'=4,'lat_1'=2,'lat_2'=4,'lat_3'=2] {'feat'}, dimensions={0} | all-to-all | bytes 2097152 | tf_op jit(solution)/shard_map/all_to_all | solution.py:19
  383.6 14.7 %all_to_all.59 = f32[8,1,1024]{2,1,0:T(1,128)S(1)} all-to-all(f32[8,1,1024]{2,1,0:T(1,128)S(1)} %broadcast_in_dim.21), channel_id=1, replica_groups=mesh['feat'=8,'lat_0'=4,'lat_1'=2,'lat_2'=4,'lat_3'=2] {'feat'}, dimensions={0} | all-to-all | bytes 65536 | tf_op jit(solution)/shard_map/all_to_all | solution.py:31
  398.3 1.1 broadcast_in_dim.20
  399.4 4.4 all-to-all-start.8
  404.3 1.7 fusion.14
  407.2 46.2 %all-to-all-done.8 = bf16[8,64,1024]{2,1,0:T(8,128)(2,1)} async-done(((bf16[8,64,1024]{2,1,0:T(8,128)(2,1)}), bf16[8,64,1024]{2,1,0:T(8,128)(2,1)}, u32[]{:S(2)}, u32[]{:S(2)}) %all-to-all-start.8) | async-done | bytes 1048608 | tf_op jit(solution)/shard_map/all_to_all | solution.py:31
  453.4 2.7 fusion.1
  456.1 1.4 fusion
  457.5 2.4 copy.38
  (30 shorter events, 4.2 us)
Async XLA Ops:
  0.6 53.1 %copy-start = (bf16[2,512,1024]{2,1,0:T(8,128)(2,1)S(1)}, bf16[2,512,1024]{2,1,0:T(8,128)(2,1)}, u32[]{:S(2)}) copy-start(bf16[2,512,1024]{2,1,0:T(8,128)(2,1)} %param.5) | copy-start | bytes 6291460
  55.2 83.4 %copy-start.6 = (f32[1024]{0:T(1024)S(1)}, f32[1024]{0:T(1024)}, u32[]{:S(2)}) copy-start(f32[1024]{0:T(1024)} %param.6) | copy-start | bytes 12292
  193.8 1.3 copy-start.2
  314.8 0.7 copy-start.5
  315.5 1.6 copy-start.1
  399.4 54.0 %all-to-all-start.8 = ((bf16[8,64,1024]{2,1,0:T(8,128)(2,1)}), bf16[8,64,1024]{2,1,0:T(8,128)(2,1)}, u32[]{:S(2)}, u32[]{:S(2)}) async-start(bf16[8,64,1024]{2,1,0:T(8,128)(2,1)} %broadcast_in_dim.20), calls=%async_computation.8 | async-start | bytes 2097152 | tf_op jit(solution)/shard_map/all_to_all | solution.py:31
  453.4 2.7 copy-start.3
  453.4 2.7 copy-start.4
